TPU v7x, 32 devices: a whole 2x2x4 slice. The times are simulated.
32 devices in a mesh: grp: 2 (over x), samp: 16 (over z, y, core).
Axes of the slice: x: 2, y: 2, z: 4, core: 2. Of those that a mesh axis runs over, the one named last changes fastest.
Arguments:
- genotypes: int32 [32768, 2048], P(('grp', 'samp')), parts along dimension 0, may hold values from 0 to 2
- probe_signs: int32 [32, 32768], P(None, ('grp', 'samp')), parts along dimension 1, may hold values from 0 to 1
- phenotype: float32 [32768], P(('grp', 'samp')), parts along dimension 0, may hold values from -6 to 6
- marker_mean: float32 [2048], replicated, may hold values from 0.2 to 1.8
- marker_scale: float32 [2048], replicated, may hold values from 0.5 to 4
- marker_bin: int32 [2048], replicated, may hold values from 0 to 15, as said below
Outputs:
- products: float32 [16, 33, 32768], P(None, None, ('grp', 'samp')), parts along dimension 2
- gram: float32 [32, 16, 33], P('grp'), parts along dimension 0
There are 2 independent parts, one for each index of `grp`. A program takes and returns all parts, laid end to end along the dimension named above; an argument that names none is the same for every part. Nothing has to cross between parts.
Inputs may be any that keep to these rules, and one draw needn't show every extreme that they name: `marker_bin`: every bin holds exactly 128 markers.
All inputs are finite; a program needn't handle non-finite values.
Results may differ from a plain program's by a relative error of at most 0.0001.
Values sent between devices are 32-bit elements; how exact they have to be, the bound alone decides.
A program may use at most 128 MiB of HBM per device.

v0:
```python
import jax
import jax.numpy as jnp
from jax import lax
from jax.sharding import PartitionSpec as P

BINS = 16
M_BIN = 128


def shards(genotypes, probe_signs, phenotype, marker_mean, marker_scale, marker_bin):
    samples = genotypes.shape[0]
    devices = lax.axis_size("samp")
    total = jnp.float32(samples * devices)
    order = jnp.argsort(marker_bin, stable=True)
    picked = jnp.take(genotypes, order, axis=1).astype(jnp.float32)
    standard = (picked - marker_mean[order]) * marker_scale[order]
    vectors = jnp.concatenate(
        [(2 * probe_signs - 1).astype(jnp.float32), phenotype[None, :]], axis=0
    )
    share = lax.psum_scatter(
        jnp.dot(
            standard.T,
            vectors.T,
            precision=lax.Precision.HIGHEST,
            preferred_element_type=jnp.float32,
        ),
        "samp",
        scatter_dimension=0,
        tiled=True,
    )
    scores = lax.all_gather(share, "samp", axis=0, tiled=True)
    scores = scores / jnp.sqrt(total)
    blocks = standard.reshape(samples, BINS, M_BIN)
    weights = scores.reshape(BINS, M_BIN, scores.shape[1])
    products = jnp.einsum(
        "skm,kmr->krs", blocks, weights, precision=lax.Precision.HIGHEST
    ) / jnp.sqrt(jnp.float32(M_BIN))
    local_gram = jnp.einsum("krs,lrs->klr", products, products, precision=lax.Precision.HIGHEST)
    gram = lax.psum(local_gram, "samp") / total
    return (products, gram)


def solution(mesh):
    in_specs = (
        P(("grp", "samp"), None),
        P(None, ("grp", "samp")),
        P(("grp", "samp")),
        P(),
        P(),
        P(),
    )
    out_specs = (P(None, None, ("grp", "samp")), P("grp", None, None))
    return jax.shard_map(shards, mesh=mesh, in_specs=in_specs, out_specs=out_specs, check_vma=False)
```

profile of v0, /device:TPU:0, one launch (start us, length us, event | category | flops | bytes accessed | tf_op | source)
XLA Modules:
  0.0 233.8 jit_solution(9177498620670587703)
XLA Ops:
  7.2 0.0 copy-start
  7.2 0.0 copy-start.1
  7.2 0.0 reduce-scatter.2.cloned.1.call-start
  7.2 5.7 %sort.17 = (s32[2048]{0:T(1024)}, s32[2048]{0:T(1024)S(1)}) sort(s32[2048]{0:T(1024)} %param.11, s32[2048]{0:T(1024)S(1)} %iota.4), dimensions={0}, to_apply=%region_0.0 | sort | flops 22528 | bytes 32768 | tf_op jit(solution)/shard_map/jit(argsort)/sort | solution.py:14
  13.0 0.0 copy-done
  13.0 0.0 copy-start.3
  13.0 11.8 %gather_fusion.2 = f32[2048]{0:T(1024)S(1)} fusion(f32[2048]{0:T(1024)S(1)} %copy-done, s32[2048]{0:T(1024)S(1)} %fusion.25), kind=kCustom, calls=%fused_computation.2 | custom fusion | bytes 24576 | tf_op jit(solution)/shard_map/gather | solution.py:16
  24.8 0.0 copy-done.1
  24.8 11.8 %gather_fusion.1 = f32[2048]{0:T(1024)S(1)} fusion(f32[2048]{0:T(1024)S(1)} %copy-done.1, s32[2048]{0:T(1024)S(1)} %fusion.25), kind=kCustom, calls=%fused_computation.1 | custom fusion | bytes 24576 | tf_op jit(solution)/shard_map/gather | solution.py:16
  36.6 0.0 copy-done.3
  36.6 9.3 %copy.15 = s32[1024,2048]{0,1:T(8,128)} copy(s32[1024,2048]{1,0:T(8,128)} %param.6) | data formatting | bytes 16777216 | tf_op args[0]
  45.9 0.0 copy-start.4
  45.9 15.1 %gather_fusion = s32[2048,1024]{1,0:T(8,128)} fusion(s32[1024,2048]{0,1:T(8,128)} %copy.15, s32[2048]{0:T(1024)S(1)} %fusion.25), kind=kCustom, calls=%fused_computation | custom fusion | bytes 16785408 | tf_op jit(solution)/shard_map/jit(_take)/gather | solution.py:15
  61.1 0.0 copy-done.4
  61.1 12.3 %fusion.3 = f32[2048,33]{0,1:T(8,128)} fusion(s32[2048,1024]{1,0:T(8,128)} %gather_fusion, f32[2048]{0:T(1024)S(1)} %gather_fusion.2, f32[2048]{0:T(1024)S(1)} %gather_fusion.1, pred[2048]{0:T(1024)(128)(4,1)S(1)} %compare_and_fusion, f32[1,1024]{1,0:T(1,128)S(1)} %bitcast.31, f32[32,1024]{1,0:T(8,128)S(1)} %add_convert_fusion), kind=kOutput, calls=%fused_computation.7 | convolution fusion | flops 838894592 | bytes 8812544 | tf_op jit(solution)/shard_map/dot_general | solution.py:21
  73.3 0.0 reduce-scatter.2.cloned.1.call-update
  73.4 9.3 %copy.16 = s32[1024,16,128]{2,0,1:T(8,128)} copy(s32[1024,16,128]{0,2,1:T(8,128)} %bitcast.26) | data formatting | bytes 16777216 | tf_op jit(solution)/shard_map/jit(_take)/gather | solution.py:15
  82.6 45.9 %reduce-scatter.2.cloned.1.call-done = f32[128,33]{0,1:T(8,128)} async-done(((f32[2048,33]{0,1:T(8,128)}), f32[128,33]{0,1:T(8,128)}) %reduce-scatter.2.cloned.1.call-update) | async-done | bytes 16912 | tf_op jit(solution)/shard_map/reduce_scatter | solution.py:20
  128.6 20.7 %all_gather.3 = f32[2048,33]{0,1:T(8,128)S(1)} all-gather(f32[128,33]{0,1:T(8,128)} %reduce-scatter.2.cloned.1.call-done), channel_id=1, replica_groups=mesh['grp'=2,'samp'=16] {'samp'}, dimensions={0}, use_global_device_ids=true | all-gather | bytes 287232 | tf_op jit(solution)/shard_map/all_gather | solution.py:31
  149.3 0.1 copy.22
  149.4 11.3 %fusion.18 = f32[16,33,1024]{2,1,0:T(8,128)S(1)} fusion(s32[1024,16,128]{2,0,1:T(8,128)} %copy.16, f32[16,128]{1,0:T(8,128)S(1)} %bitcast.29, f32[16,128]{1,0:T(8,128)S(1)} %bitcast.30, pred[16,128]{1,0:T(8,128)(4,1)S(1)} %fusion.31, f32[16,128,33]{1,0,2:T(8,128)S(1)} %slice_bitcast_fusion), kind=kOutput, calls=%fused_computation.21 | convolution fusion | flops 839401472 | bytes 10840064 | tf_op jit(solution)/shard_map/skm,kmr->krs/dot_general | solution.py:35
  160.7 1.3 copy.20
  161.9 0.0 copy-start.2
  162.0 3.1 %convolution_bitcast_fusion = f32[16,16,33]{0,1,2:T(8,128)S(1)} fusion(f32[16,33,1024]{2,0,1:T(8,128)S(1)} %copy.20), kind=kOutput, calls=%fused_computation.22 | convolution fusion | flops 103809024 | bytes 2196480 | tf_op jit(solution)/shard_map/krs,lrs->klr/dot_general | solution.py:38
  165.1 61.0 %psum.7 = f32[16,16,33]{0,1,2:T(8,128)S(1)} all-reduce(f32[16,16,33]{0,1,2:T(8,128)S(1)} %convolution_bitcast_fusion), channel_id=1, replica_groups=mesh['grp'=2,'samp'=16] {'samp'}, use_global_device_ids=true, to_apply=%region_2.3 | all-reduce | flops 8448 | bytes 67584 | tf_op jit(solution)/shard_map/psum | solution.py:39
  226.1 0.8 copy.21
  227.0 0.0 copy-done.2
  (8 shorter events, 0.1 us)
Async XLA Ops:
  7.2 5.8 %copy-start = (f32[2048]{0:T(1024)S(1)}, f32[2048]{0:T(1024)}, u32[]{:S(2)}) copy-start(f32[2048]{0:T(1024)} %param.10) | copy-start | bytes 24580
  7.2 17.6 %copy-start.1 = (f32[2048]{0:T(1024)S(1)}, f32[2048]{0:T(1024)}, u32[]{:S(2)}) copy-start(f32[2048]{0:T(1024)} %param.9) | copy-start | bytes 24580
  7.2 121.4 %reduce-scatter.2.cloned.1.call-start = ((), (), s32[]{:S(2)}) async-start(), calls=%async_computation.1 | async-start | bytes 348160 | tf_op jit(solution)/shard_map/reduce_scatter | solution.py:20
  13.0 23.6 %copy-start.3 = (s32[32,1024]{1,0:T(8,128)S(1)}, s32[32,1024]{1,0:T(8,128)}, u32[]{:S(2)}) copy-start(s32[32,1024]{1,0:T(8,128)} %param.7) | copy-start | bytes 393220
  45.9 15.2 %copy-start.4 = (f32[1024]{0:T(1024)S(1)}, f32[1024]{0:T(1024)}, u32[]{:S(2)}) copy-start(f32[1024]{0:T(1024)} %param.8) | copy-start | bytes 12292
  161.9 65.0 %copy-start.2 = (f32[16,33,1024]{2,0,1:T(8,128)}, f32[16,33,1024]{2,0,1:T(8,128)S(1)}, u32[]{:S(2)}) copy-start(f32[16,33,1024]{2,0,1:T(8,128)S(1)} %copy.20) | copy-start | bytes 6488068
Sparse Core Ops, SparseCore 0:
  73.5 55.0 reduce-scatter.1
where the time goes:
time: 234 us
  blocking collectives  81.7 us (35%)
  local copies, waits for them, and re-layouts  59.5 us (25%)
  waiting for transfers between devices  45.9 us (20%)
  matrix products  26.7 us (11%)
  between operations  14.2 us (6%)
  other arithmetic  5.82 us (2%)
    psum x1, blocking collectives, shards(): gram = lax.psum(local_gram, 'samp') / total  61 us
    reduce_scatter x1, waiting for transfers between devices, shards(): lax.psum_scatter(jnp.dot(standard.T, vectors.T, precision=lax.Precision.H...  45.9 us
    gather x2, local copies, waits for them, and re-layouts, shards(): picked = jnp.take(genotypes, order, axis=1).astype(jnp.float32)  24.4 us
    gather x2, local copies, waits for them, and re-layouts, shards(): standard = (picked - marker_mean[order]) * marker_scale[order]  23.6 us
    all_gather x1, blocking collectives, shards(): scores = lax.all_gather(share, 'samp', axis=0, tiled=True)  20.7 us
    dot_general x1, matrix products, shards(): jnp.dot(standard.T, vectors.T, precision=lax.Precision.HIGHEST, preferred...  12.3 us
    unnamed x14, local copies, waits for them, and re-layouts  11.5 us
    dot_general x1, matrix products, shards(): jnp.einsum('skm,kmr->krs', blocks, weights, precision=lax.Precision.HIGHEST)  11.3 us
  transfers between devices with their start and end apart: 1, of which 1 were waited for; matrix products, arithmetic and copies ran while one was open for 4% of the time, Pallas kernels for 0%

commit v1 on v0

v1 whole, which is shorter than its diff:
```python
import functools
import math

import jax
import jax.numpy as jnp
from jax import lax
from jax.experimental import pallas as pl
from jax.experimental.pallas import tpu as pltpu
from jax.sharding import PartitionSpec as P

BINS = 16
M_BIN = 128
LANES = 128
GROUP = 256
BF = jnp.bfloat16
F32 = jnp.float32
MESH = pl.DeviceIdType.MESH
NT = (((1,), (1,)), ((), ()))


def dot(a, b):
    return jnp.dot(a, b, preferred_element_type=F32)


def dot_nt(a, b):
    return lax.dot_general(a, b, NT, preferred_element_type=F32)


def high(x):
    return x.astype(BF)


def rest(x):
    return (x - x.astype(BF).astype(F32)).astype(BF)


def kernel(n, split, rows, per, total, g_hbm, probe, pheno, mean, scale, bins, out_hbm, gram,
           gbuf, gb, vec, tsend, sibrecv, rsend, rsrecv, ag, wsp, prods, gsend, grecv, gsum,
           in_sem, out_sem, sib_s, sib_r, rs_s, rs_r, ag_s, ag_r, fwd_s, gr_s, gr_r, ga_s, ga_r):
    me = lax.axis_index("samp")
    chip, core = me // 2, me % 2
    chips = n // 2
    sib = me + 1 - 2 * core
    samples, markers = g_hbm.shape
    probes = probe.shape[0]
    vecs = probes + 1
    groups = markers // GROUP
    home = chip // split

    barrier = pltpu.get_barrier_semaphore()

    @pl.loop(1, n)
    def _(s):
        pl.semaphore_signal(barrier, inc=1, device_id={"samp": lax.rem(me + s, n)}, device_id_type=MESH)

    def cg_of(q):
        return lax.rem(home + 1 + q, groups)

    def cols(q):
        return pl.ds(pl.multiple_of(cg_of(q) * GROUP, GROUP), GROUP)

    def load(q):
        return pltpu.make_async_copy(g_hbm.at[:, cols(q)], gbuf.at[q], in_sem.at[q])

    for q in range(groups):
        load(q).start()

    def to_sib(m):
        return pltpu.make_async_remote_copy(
            tsend.at[m, 1 - core], sibrecv.at[m], sib_s.at[m], sib_r.at[m],
            device_id={"samp": sib}, device_id_type=MESH)

    def to_owner(m):
        return pltpu.make_async_remote_copy(
            rsend.at[m], rsrecv.at[chip], rs_s.at[m], rs_r.at[chip],
            device_id={"samp": 2 * m + core}, device_id_type=MESH)

    def from_owner(m):
        return pltpu.make_async_remote_copy(
            rsend.at[m], rsrecv.at[m], rs_s.at[m], rs_r.at[m],
            device_id={"samp": 2 * m + core}, device_id_type=MESH)

    signs = (2 * probe[...] - 1).astype(F32)
    ph = pheno[...]
    ph_mid = ph - high(ph).astype(F32)
    vec[0:probes, :] = high(signs)
    tail = jnp.concatenate(
        [ph, ph_mid, ph_mid - high(ph_mid).astype(F32), jnp.zeros((13, samples), F32)], axis=0)
    vec[probes:probes + 16, :] = high(tail)
    sum_p = jnp.sum(signs, axis=1, keepdims=True)
    sum_y = jnp.sum(ph, axis=1, keepdims=True)

    def combine(q):
        for i in range(split):
            m = cg_of(q) * split + i
            to_sib(m).wait_recv()
            both = tsend[m, core] + sibrecv[m]
            if split == 1:
                if q == groups - 1:
                    rsrecv[m] = both
                else:
                    rsend[m] = both
                    to_owner(m).start()
            else:
                @pl.when(m == chip)
                def _():
                    rsrecv[m] = both

                @pl.when(m != chip)
                def _():
                    rsend[m] = both
                    to_owner(m).start()

    for q in range(groups):
        load(q).wait()
        part = gbuf[q].astype(F32).astype(BF)
        gb[:, cols(q)] = part
        t = dot(vec[...], part)
        mu = mean[:, cols(q)]
        tp = t[0:probes] - sum_p * mu
        ty = t[probes:probes + 1] + t[probes + 1:probes + 2] + t[probes + 2:probes + 3] - sum_y * mu
        cg = cg_of(q)
        if split == 1:
            for h in range(2):
                at = slice(h * LANES, (h + 1) * LANES)
                tsend[cg, h, 0:probes, :] = tp[:, at]
                tsend[cg, h, probes:vecs, :] = ty[:, at]
        else:
            whole = jnp.concatenate([tp, ty, jnp.zeros((split * rows - vecs, GROUP), F32)], axis=0)
            for h in range(2):
                for s in range(split):
                    tsend[cg * split + (h * split + s) // 2, s % 2] = whole[
                        s * rows:(s + 1) * rows, h * LANES:(h + 1) * LANES]
        if q == 0:
            pl.semaphore_wait(barrier, n - 1)
        for i in range(split):
            to_sib(cg * split + i).start()
        if q > 0:
            combine(q - 1)
    combine(groups - 1)

    def others(body):
        @pl.loop(1, chips)
        def _(s):
            body(lax.rem(chip + s, chips))

    others(lambda m: from_owner(m).wait_recv())
    ag[me] = jnp.sum(rsrecv[...], axis=0)

    def ag_chip(m):
        return pltpu.make_async_remote_copy(
            ag.at[me], ag.at[me], ag_s.at[m], ag_r.at[me],
            device_id={"samp": 2 * m + core}, device_id_type=MESH)

    def ag_fwd(m):
        return pltpu.make_async_remote_copy(
            ag.at[2 * m + core], ag.at[2 * m + core], fwd_s.at[m], ag_r.at[2 * m + core],
            device_id={"samp": sib}, device_id_type=MESH)

    def ag_got(d):
        return pltpu.make_async_remote_copy(
            ag.at[d], ag.at[d], fwd_s.at[chip], ag_r.at[d],
            device_id={"samp": sib}, device_id_type=MESH)

    others(lambda m: ag_chip(m).start())
    ag_fwd(chip).start()

    def pass_on(m):
        ag_got(2 * m + core).wait_recv()
        ag_fwd(m).start()

    others(pass_on)

    @pl.loop(0, chips)
    def _(s):
        ag_got(2 * lax.rem(chip + s, chips) + 1 - core).wait_recv()

    factor = 1.0 / (math.sqrt(total) * math.sqrt(M_BIN))
    if split == 1:
        got = jnp.concatenate([ag[d] for d in range(n)], axis=1)
    else:
        got = jnp.concatenate(
            [jnp.concatenate([ag[lane * split + s] for s in range(split)], axis=0)[0:vecs]
             for lane in range(n // split)], axis=1)
    sc = scale[...]
    w = got * (sc * sc * factor)
    wh, wl = high(w).astype(F32), rest(w).astype(F32)
    wm = (wh + wl) * mean[...]
    member = lax.broadcasted_iota(jnp.int32, (BINS, markers), 0) == bins[...]
    offs = []
    for r in range(vecs):
        at = slice(r * BINS, (r + 1) * BINS)
        wsp[0, at, :] = high(jnp.where(member, wh[r:r + 1], 0.0))
        wsp[1, at, :] = high(jnp.where(member, wl[r:r + 1], 0.0))
        offs.append(jnp.sum(jnp.where(member, wm[r:r + 1], 0.0), axis=1, keepdims=True))
    off = jnp.concatenate(offs, axis=0)
    half = (probes // 2) * BINS
    cuts = [(0, half), (half, 2 * half), (2 * half, vecs * BINS)]
    accs = [jnp.zeros((b - a, b - a), F32) for a, b in cuts]
    for nb in range(samples // GROUP):
        at = slice(nb * GROUP, (nb + 1) * GROUP)
        gpart = gb[at, :]
        res = dot_nt(wsp[0], gpart) + dot_nt(wsp[1], gpart) - off
        prods[:, :, at] = res.reshape(vecs, BINS, GROUP)
        hi, lo = high(res), rest(res)
        for i, (a, b) in enumerate(cuts):
            h, l = hi[a:b], lo[a:b]
            accs[i] = accs[i] + dot_nt(h, h) + dot_nt(h, l) + dot_nt(l, h)

    def out_copy(r):
        return pltpu.make_async_copy(prods.at[r], out_hbm.at[:, r, :], out_sem.at[r])

    @pl.loop(0, vecs)
    def _(r):
        out_copy(r).start()

    strips = []
    for acc in accs:
        size = acc.shape[0]
        same = (lax.broadcasted_iota(jnp.int32, (size, size), 0) // BINS
                == lax.broadcasted_iota(jnp.int32, (size, size), 1) // BINS)
        strips.append(jnp.sum(jnp.where(same, acc, 0.0).reshape(size // BINS, BINS, size), axis=0))
    strips.append(jnp.zeros((BINS, LANES - BINS), F32))
    flat = jnp.concatenate(strips, axis=1)
    width = flat.shape[1] // LANES
    for k in range(BINS):
        for t in range(width):
            p = k * width + t
            gsend[p // per, p % per:p % per + 1, :] = flat[k:k + 1, t * LANES:(t + 1) * LANES]
    for p in range(BINS * width, n * per):
        gsend[p // per, p % per:p % per + 1, :] = jnp.zeros((1, LANES), F32)

    def gr(d, slot):
        return pltpu.make_async_remote_copy(
            gsend.at[d], grecv.at[slot], gr_s.at[d], gr_r.at[slot],
            device_id={"samp": d}, device_id_type=MESH)

    def ga(d, slot):
        return pltpu.make_async_remote_copy(
            gsum.at[slot], gsum.at[slot], ga_s.at[d], ga_r.at[slot],
            device_id={"samp": d}, device_id_type=MESH)

    def peers(body):
        @pl.loop(1, n)
        def _(s):
            body(lax.rem(me + s, n))

    peers(lambda d: gr(d, me).start())
    grecv[me] = gsend[me]
    peers(lambda d: gr(d, d).wait_recv())
    gsum[me] = jnp.sum(grecv[...], axis=0) * (1.0 / total)
    peers(lambda d: ga(d, me).start())
    peers(lambda d: ga(d, d).wait_recv())
    gram[...] = gsum[...]

    def finish(d):
        gr(d, me).wait_send()
        ga(d, me).wait_send()

    peers(finish)

    def finish_chip(m):
        to_owner(m).wait_send()
        ag_chip(m).wait_send()

    others(finish_chip)

    @pl.loop(0, chips)
    def _(m):
        to_sib(m).wait_send()
        ag_fwd(m).wait_send()

    @pl.loop(0, vecs)
    def _(r):
        out_copy(r).wait()


def shards(genotypes, probe_signs, phenotype, marker_mean, marker_scale, marker_bin):
    samples, markers = genotypes.shape
    probes = probe_signs.shape[0]
    vecs = probes + 1
    n = lax.axis_size("samp")
    total = float(samples * n)
    chunks = markers // LANES
    split = n // chunks
    rows = -(-vecs // split)
    width = -(-(vecs * BINS) // LANES)
    per = -(-(BINS * width) // n)
    chips = n // 2
    groups = markers // GROUP
    vm = pltpu.VMEM
    dma = pltpu.SemaphoreType.DMA
    vspec = pl.BlockSpec(memory_space=pltpu.VMEM)
    anyspec = pl.BlockSpec(memory_space=pl.ANY)
    products, gram = pl.pallas_call(
        functools.partial(kernel, n, split, rows, per, total),
        out_shape=(jax.ShapeDtypeStruct((BINS, vecs, samples), F32),
                   jax.ShapeDtypeStruct((n, per, LANES), F32)),
        in_specs=[anyspec] + [vspec] * 5,
        out_specs=(anyspec, vspec),
        scratch_shapes=[
            vm((groups, samples, GROUP), jnp.int32),
            vm((samples, markers), BF),
            vm((probes + 16, samples), BF),
            vm((chips, 2, rows, LANES), F32),
            vm((chips, rows, LANES), F32),
            vm((chips, rows, LANES), F32),
            vm((chips, rows, LANES), F32),
            vm((n, rows, LANES), F32),
            vm((2, vecs * BINS, markers), BF),
            vm((vecs, BINS, samples), F32),
            vm((n, per, LANES), F32),
            vm((n, per, LANES), F32),
            vm((n, per, LANES), F32),
            dma((groups,)), dma((vecs,)),
            dma((chips,)), dma((chips,)), dma((chips,)), dma((chips,)),
            dma((chips,)), dma((n,)), dma((chips,)),
            dma((n,)), dma((n,)), dma((n,)), dma((n,)),
        ],
        compiler_params=pltpu.CompilerParams(
            collective_id=0, has_side_effects=True, vmem_limit_bytes=60 * 1024 * 1024),
    )(genotypes, probe_signs, phenotype[None, :], marker_mean[None, :],
      marker_scale[None, :], marker_bin[None, :])
    gram = gram.reshape(n * per, LANES)[:BINS * width].reshape(BINS, width * LANES)
    gram = gram[:, :vecs * BINS].reshape(BINS, vecs, BINS).transpose(0, 2, 1)
    return products, gram


def solution(mesh):
    in_specs = (
        P(("grp", "samp"), None),
        P(None, ("grp", "samp")),
        P(("grp", "samp")),
        P(),
        P(),
        P(),
    )
    out_specs = (P(None, None, ("grp", "samp")), P("grp", None, None))
    return jax.shard_map(shards, mesh=mesh, in_specs=in_specs, out_specs=out_specs, check_vma=False)
```

time: 234 us -> 46.9 us (0.20)
  blocking collectives: 81.7 us -> 0 us
  local copies, waits for them, and re-layouts: 59.5 us -> 5.34 us
  waiting for transfers between devices: 45.9 us -> 0 us
  Pallas kernels: 0 us -> 40.7 us
  matrix products: 26.7 us -> 0 us
  between operations: 14.2 us -> 0.66 us
  other arithmetic: 5.82 us -> 0 us
    psum x1 -> x0, blocking collectives: 61 us -> none  [shards(): gram = lax.psum(local_gram, 'samp') / total]
    gather x4 -> x0, local copies, waits for them, and re-layouts: 48 us -> none  [the longest x2 24.4 us: shards(): picked = jnp.take(genotypes, order, axis=1).astype(jnp.float32)]
    reduce_scatter x1 -> x0, waiting for transfers between devices: 45.9 us -> none  [shards(): lax.psum_scatter(jnp.dot(standard.T, vectors.T, precision=lax.Precision.H...]
    pallas_call x0 -> x1, Pallas kernels: none -> 40.7 us  [shards(): pl.pallas_call(functools.partial(kernel, n, split, rows, per, total), out...]
    dot_general x3 -> x0, matrix products: 26.7 us -> none  [the longest x1 12.3 us: shards(): jnp.dot(standard.T, vectors.T, precision=lax.Precision.HIGHEST, preferred...]
    all_gather x1 -> x0, blocking collectives: 20.7 us -> none  [shards(): scores = lax.all_gather(share, 'samp', axis=0, tiled=True)]
    unnamed x14 -> x5, local copies, waits for them, and re-layouts: 11.5 us -> 5.21 us
    sort x1 -> x0, other arithmetic: 5.74 us -> none  [shards(): order = jnp.argsort(marker_bin, stable=True)]
  transfers between devices with their start and end apart: 1 -> 0, of which waited for: 1 -> 0; matrix products, arithmetic and copies ran while one was open for 4% -> 0% of each run, Pallas kernels for 0% -> 0%
where the time goes in v1:
time: 46.9 us; the launch traced here: 46.7 us
  Pallas kernels  40.7 us (87%)
  local copies, waits for them, and re-layouts  5.34 us (11%)
  between operations  0.66 us (1%)
    pallas_call x1, Pallas kernels, shards(): pl.pallas_call(functools.partial(kernel, n, split, rows, per, total), out...  40.7 us
    unnamed x5, local copies, waits for them, and re-layouts  5.21 us

profile of v1, /device:TPU:0, one launch (start us, length us, event | category | flops | bytes accessed | tf_op | source)
XLA Modules:
  0.0 46.7 jit_solution(6055468623059557551)
XLA Ops:
  0.6 40.7 %shard_map.77 = (f32[16,33,1024]{2,1,0:T(8,128)}, f32[16,5,128]{2,1,0:T(8,128)}) custom-call(s32[1024,2048]{1,0:T(8,128)} %g_hbm.1, s32[32,1024]{1,0:T(8,128)} %probe.1, f32[1,1024]{1,0:T(1,128)} %bitcast.16, f32[1,2048]{1,0:T(1,128)} %bitcast.13, f32[1,2048]{1,0:T(1,128)} %bitcast.14, s32[1,2048]{1,0:T(1,128)} %bitcast.15), custom_call_target="tpu_custom_call" | custom-call | tf_op jit(solution)/shard_map/pallas_call | solution.py:295
  41.4 0.0 copy-start
  41.4 4.4 %copy.9 = f32[16,33,1024]{2,0,1:T(8,128)} copy(f32[16,33,1024]{2,1,0:T(8,128)} %get-tuple-element.8) | data formatting | bytes 4325376
  45.8 0.0 copy-done
  45.8 0.1 reshape.7
  45.9 0.8 %copy.10 = f32[16,16,33]{2,1,0:T(8,128)} copy(f32[16,16,33]{1,2,0:T(8,128)S(1)} %bitcast.10) | data formatting | bytes 67584
  (1 shorter events, 0.0 us)
Async XLA Ops:
  41.4 4.4 %copy-start = (f32[16,5,128]{2,1,0:T(8,128)S(1)}, f32[16,5,128]{2,1,0:T(8,128)}, u32[]{:S(2)}) copy-start(f32[16,5,128]{2,1,0:T(8,128)} %get-tuple-element.5) | copy-start | bytes 122884

commit v2 on v1

--- a/solution.py
+++ b/solution.py
@@ -35,7 +35,7 @@
 
 
 def kernel(n, split, rows, per, total, g_hbm, probe, pheno, mean, scale, bins, out_hbm, gram,
-           gbuf, gb, vec, tsend, sibrecv, rsend, rsrecv, ag, wsp, prods, gsend, grecv, gsum,
+           gbuf, gb, vec, tsend, sibrecv, rsend, rsrecv, ag, wsp, prods, offs, gsend, grecv, gsum,
            in_sem, out_sem, sib_s, sib_r, rs_s, rs_r, ag_s, ag_r, fwd_s, gr_s, gr_r, ga_s, ga_r):
     me = lax.axis_index("samp")
     chip, core = me // 2, me % 2
@@ -165,54 +165,73 @@
     others(lambda m: ag_chip(m).start())
     ag_fwd(chip).start()
 
-    def pass_on(m):
-        ag_got(2 * m + core).wait_recv()
-        ag_fwd(m).start()
-
-    others(pass_on)
-
-    @pl.loop(0, chips)
+    factor = 1.0 / (math.sqrt(total) * math.sqrt(M_BIN))
+    depth = vecs * BINS
+    prods[...] = jnp.zeros_like(prods)
+    offs[...] = jnp.zeros_like(offs)
+
+    def receive(s):
+        for i in range(split):
+            m = lax.rem(home + s, groups) * split + i
+
+            @pl.when(m != chip)
+            def _():
+                ag_got(2 * m + core).wait_recv()
+                ag_fwd(m).start()
+
+    def multiply(s):
+        cg = lax.rem(home + s, groups)
+        for i in range(split):
+            ag_got(2 * (cg * split + i) + 1 - core).wait_recv()
+        at = pl.ds(pl.multiple_of(cg * GROUP, GROUP), GROUP)
+        lanes = []
+        for h in range(2):
+            first = (2 * cg + h) * split
+            part = [ag[first + i] for i in range(split)]
+            lanes.append(part[0] if split == 1 else jnp.concatenate(part, axis=0)[0:vecs])
+        sc = scale[:, at]
+        w = jnp.concatenate(lanes, axis=1) * (sc * sc * factor)
+        wh, wl = high(w).astype(F32), rest(w).astype(F32)
+        wm = (wh + wl) * mean[:, at]
+        member = lax.broadcasted_iota(jnp.int32, (BINS, GROUP), 0) == bins[:, at]
+        for r in range(vecs):
+            row = slice(r * BINS, (r + 1) * BINS)
+            wsp[row, :] = high(jnp.where(member, wh[r:r + 1], 0.0))
+            wsp[depth + r * BINS:depth + (r + 1) * BINS, :] = high(jnp.where(member, wl[r:r + 1], 0.0))
+            o = jnp.where(member, wm[r:r + 1], 0.0)
+            offs[row, :] += o[:, :LANES] + o[:, LANES:]
+        for nb in range(samples // GROUP):
+            span = slice(nb * GROUP, (nb + 1) * GROUP)
+            res = dot_nt(wsp[...], gb[span, at])
+            prods[:, span] += res[:depth] + res[depth:]
+
+    if split > 1:
+        receive(0)
+
+    @pl.loop(1, groups)
     def _(s):
-        ag_got(2 * lax.rem(chip + s, chips) + 1 - core).wait_recv()
-
-    factor = 1.0 / (math.sqrt(total) * math.sqrt(M_BIN))
-    if split == 1:
-        got = jnp.concatenate([ag[d] for d in range(n)], axis=1)
-    else:
-        got = jnp.concatenate(
-            [jnp.concatenate([ag[lane * split + s] for s in range(split)], axis=0)[0:vecs]
-             for lane in range(n // split)], axis=1)
-    sc = scale[...]
-    w = got * (sc * sc * factor)
-    wh, wl = high(w).astype(F32), rest(w).astype(F32)
-    wm = (wh + wl) * mean[...]
-    member = lax.broadcasted_iota(jnp.int32, (BINS, markers), 0) == bins[...]
-    offs = []
-    for r in range(vecs):
-        at = slice(r * BINS, (r + 1) * BINS)
-        wsp[0, at, :] = high(jnp.where(member, wh[r:r + 1], 0.0))
-        wsp[1, at, :] = high(jnp.where(member, wl[r:r + 1], 0.0))
-        offs.append(jnp.sum(jnp.where(member, wm[r:r + 1], 0.0), axis=1, keepdims=True))
-    off = jnp.concatenate(offs, axis=0)
+        receive(s)
+        multiply(s - 1)
+
+    multiply(groups - 1)
+    off = jnp.sum(offs[...], axis=1, keepdims=True)
     half = (probes // 2) * BINS
-    cuts = [(0, half), (half, 2 * half), (2 * half, vecs * BINS)]
+    cuts = [(0, half), (half, 2 * half), (2 * half, depth)]
     accs = [jnp.zeros((b - a, b - a), F32) for a, b in cuts]
+
+    def out_copy(nb):
+        span = slice(nb * GROUP, (nb + 1) * GROUP)
+        return pltpu.make_async_copy(prods.at[:, span], out_hbm.at[:, span], out_sem.at[nb])
+
     for nb in range(samples // GROUP):
-        at = slice(nb * GROUP, (nb + 1) * GROUP)
-        gpart = gb[at, :]
-        res = dot_nt(wsp[0], gpart) + dot_nt(wsp[1], gpart) - off
-        prods[:, :, at] = res.reshape(vecs, BINS, GROUP)
+        span = slice(nb * GROUP, (nb + 1) * GROUP)
+        res = prods[:, span] - off
+        prods[:, span] = res
+        out_copy(nb).start()
         hi, lo = high(res), rest(res)
         for i, (a, b) in enumerate(cuts):
             h, l = hi[a:b], lo[a:b]
             accs[i] = accs[i] + dot_nt(h, h) + dot_nt(h, l) + dot_nt(l, h)
-
-    def out_copy(r):
-        return pltpu.make_async_copy(prods.at[r], out_hbm.at[:, r, :], out_sem.at[r])
-
-    @pl.loop(0, vecs)
-    def _(r):
-        out_copy(r).start()
 
     strips = []
     for acc in accs:
@@ -270,9 +289,8 @@
         to_sib(m).wait_send()
         ag_fwd(m).wait_send()
 
-    @pl.loop(0, vecs)
-    def _(r):
-        out_copy(r).wait()
+    for nb in range(samples // GROUP):
+        out_copy(nb).wait()
 
 
 def shards(genotypes, probe_signs, phenotype, marker_mean, marker_scale, marker_bin):
@@ -294,7 +312,7 @@
     anyspec = pl.BlockSpec(memory_space=pl.ANY)
     products, gram = pl.pallas_call(
         functools.partial(kernel, n, split, rows, per, total),
-        out_shape=(jax.ShapeDtypeStruct((BINS, vecs, samples), F32),
+        out_shape=(jax.ShapeDtypeStruct((vecs * BINS, samples), F32),
                    jax.ShapeDtypeStruct((n, per, LANES), F32)),
         in_specs=[anyspec] + [vspec] * 5,
         out_specs=(anyspec, vspec),
@@ -307,12 +325,13 @@
             vm((chips, rows, LANES), F32),
             vm((chips, rows, LANES), F32),
             vm((n, rows, LANES), F32),
-            vm((2, vecs * BINS, markers), BF),
-            vm((vecs, BINS, samples), F32),
+            vm((2 * vecs * BINS, GROUP), BF),
+            vm((vecs * BINS, samples), F32),
+            vm((vecs * BINS, LANES), F32),
             vm((n, per, LANES), F32),
             vm((n, per, LANES), F32),
             vm((n, per, LANES), F32),
-            dma((groups,)), dma((vecs,)),
+            dma((groups,)), dma((samples // GROUP,)),
             dma((chips,)), dma((chips,)), dma((chips,)), dma((chips,)),
             dma((chips,)), dma((n,)), dma((chips,)),
             dma((n,)), dma((n,)), dma((n,)), dma((n,)),
@@ -323,7 +342,7 @@
       marker_scale[None, :], marker_bin[None, :])
     gram = gram.reshape(n * per, LANES)[:BINS * width].reshape(BINS, width * LANES)
     gram = gram[:, :vecs * BINS].reshape(BINS, vecs, BINS).transpose(0, 2, 1)
-    return products, gram
+    return products.reshape(vecs, BINS, samples).transpose(1, 0, 2), gram
 
 
 def solution(mesh):

time: 46.9 us -> 42 us (0.90)
  Pallas kernels: 40.7 us -> 36.1 us
    pallas_call x1, Pallas kernels: 40.7 us -> 36.1 us  [shards(): pl.pallas_call(functools.partial(kernel, n, split, rows, per, total), out...]
    unnamed x5 -> x3, local copies, waits for them, and re-layouts: 5.21 us -> 4.89 us
where the time goes in v2:
time: 42 us; the launch traced here: 41.8 us
  Pallas kernels  36.1 us (86%)
  local copies, waits for them, and re-layouts  5.01 us (12%)
  between operations  0.65 us (2%)
    pallas_call x1, Pallas kernels, shards(): pl.pallas_call(functools.partial(kernel, n, split, rows, per, total), out...  36.1 us
    unnamed x3, local copies, waits for them, and re-layouts  4.89 us

profile of v2, /device:TPU:0, one launch (start us, length us, event | category | flops | bytes accessed | tf_op | source)
XLA Modules:
  0.0 41.8 jit_solution(3946730654944611747)
XLA Ops:
  0.6 36.1 %shard_map.77 = (f32[528,1024]{1,0:T(8,128)}, f32[16,5,128]{2,1,0:T(8,128)}) custom-call(s32[1024,2048]{1,0:T(8,128)} %g_hbm.1, s32[32,1024]{1,0:T(8,128)} %probe.1, f32[1,1024]{1,0:T(1,128)} %bitcast.20, f32[1,2048]{1,0:T(1,128)} %bitcast.17, f32[1,2048]{1,0:T(1,128)} %bitcast.18, s32[1,2048]{1,0:T(1,128)} %bitcast.19), custom_call_target="tpu_custom_call" | custom-call | tf_op jit(solution)/shard_map/pallas_call | solution.py:313
  36.8 0.8 %copy.11 = f32[2,8,5,128]{3,1,2,0:T(8,128)S(1)} copy(f32[2,8,5,128]{3,2,1,0:T(8,128)} %bitcast.16) | data formatting | bytes 81920
  37.6 0.1 reshape.11
  37.8 0.8 %copy.8 = f32[16,16,33]{2,1,0:T(8,128)} copy(f32[16,16,33]{1,2,0:T(8,128)S(1)} %bitcast.14) | data formatting | bytes 67584
  38.6 3.2 %copy.13 = f32[16,33,1024]{2,0,1:T(8,128)} copy(f32[16,33,1024]{2,0,1:T(8,128)} %bitcast.13) | data formatting | bytes 4325376

commit v3 on v2

--- a/solution.py
+++ b/solution.py
@@ -34,9 +34,10 @@
     return (x - x.astype(BF).astype(F32)).astype(BF)
 
 
-def kernel(n, split, rows, per, total, g_hbm, probe, pheno, mean, scale, bins, out_hbm, gram,
-           gbuf, gb, vec, tsend, sibrecv, rsend, rsrecv, ag, wsp, prods, offs, gsend, grecv, gsum,
-           in_sem, out_sem, sib_s, sib_r, rs_s, rs_r, ag_s, ag_r, fwd_s, gr_s, gr_r, ga_s, ga_r):
+def kernel(n, split, rows, per, total, g_hbm, probe_hbm, pheno_hbm, mean_hbm, scale_hbm, bins_hbm, prods, gram,
+           probe, pheno, mean, scale, bins,
+           gbuf, gb, vec, tsend, sibrecv, rsend, rsrecv, ag, wsp, offs, gsend, grecv, gsum,
+           small_sem, in_sem, sib_s, sib_r, rs_s, rs_r, ag_s, ag_r, fwd_s, gr_s, gr_r, ga_s, ga_r):
     me = lax.axis_index("samp")
     chip, core = me // 2, me % 2
     chips = n // 2
@@ -62,6 +63,10 @@
     def load(q):
         return pltpu.make_async_copy(g_hbm.at[:, cols(q)], gbuf.at[q], in_sem.at[q])
 
+    small = [pltpu.make_async_copy(src, dst, small_sem.at[i]) for i, (src, dst) in enumerate(
+        [(probe_hbm, probe), (pheno_hbm, pheno), (mean_hbm, mean), (scale_hbm, scale), (bins_hbm, bins)])]
+    for copy in small:
+        copy.start()
     for q in range(groups):
         load(q).start()
 
@@ -80,6 +85,8 @@
             rsend.at[m], rsrecv.at[m], rs_s.at[m], rs_r.at[m],
             device_id={"samp": 2 * m + core}, device_id_type=MESH)
 
+    for copy in small:
+        copy.wait()
     signs = (2 * probe[...] - 1).astype(F32)
     ph = pheno[...]
     ph_mid = ph - high(ph).astype(F32)
@@ -219,15 +226,10 @@
     cuts = [(0, half), (half, 2 * half), (2 * half, depth)]
     accs = [jnp.zeros((b - a, b - a), F32) for a, b in cuts]
 
-    def out_copy(nb):
-        span = slice(nb * GROUP, (nb + 1) * GROUP)
-        return pltpu.make_async_copy(prods.at[:, span], out_hbm.at[:, span], out_sem.at[nb])
-
     for nb in range(samples // GROUP):
         span = slice(nb * GROUP, (nb + 1) * GROUP)
         res = prods[:, span] - off
         prods[:, span] = res
-        out_copy(nb).start()
         hi, lo = high(res), rest(res)
         for i, (a, b) in enumerate(cuts):
             h, l = hi[a:b], lo[a:b]
@@ -289,8 +291,38 @@
         to_sib(m).wait_send()
         ag_fwd(m).wait_send()
 
-    for nb in range(samples // GROUP):
-        out_copy(nb).wait()
+
+def finisher(n, per, width, vecs, prods, gsum, out_hbm, gram, sem):
+    third = prods.shape[0] // 3
+
+    def out_copy(i):
+        return pltpu.make_async_copy(
+            prods.at[i * third:(i + 1) * third], out_hbm.at[i * third:(i + 1) * third],
+            sem.at[i])
+
+    for i in range(3):
+        out_copy(i).start()
+    if n == BINS:
+        flat = jnp.concatenate([gsum[:, t, :] for t in range(width)], axis=1)
+    else:
+        flat = jnp.concatenate(
+            [jnp.concatenate([gsum[p // per, p % per:p % per + 1, :]
+                              for p in range(k * width, (k + 1) * width)], axis=1)
+             for k in range(BINS)], axis=0)
+    lanes = width * LANES
+    col = lax.broadcasted_iota(jnp.int32, (BINS, lanes), 1)
+    mine = (col % BINS) == lax.broadcasted_iota(jnp.int32, (BINS, lanes), 0)
+    spread = jnp.concatenate([jnp.where(mine, flat[k:k + 1], 0.0) for k in range(BINS)], axis=0)
+    pick = high((lax.broadcasted_iota(jnp.int32, (lanes, LANES), 0) // BINS
+                 == lax.broadcasted_iota(jnp.int32, (lanes, LANES), 1)).astype(F32))
+    a = high(spread)
+    left = spread - a.astype(F32)
+    b = high(left)
+    c = high(left - b.astype(F32))
+    res = dot(a, pick) + dot(b, pick) + dot(c, pick)
+    gram[...] = res[:, :vecs].reshape(BINS, BINS, vecs)
+    for i in range(3):
+        out_copy(i).wait()
 
 
 def shards(genotypes, probe_signs, phenotype, marker_mean, marker_scale, marker_bin):
@@ -309,14 +341,19 @@
     vm = pltpu.VMEM
     dma = pltpu.SemaphoreType.DMA
     vspec = pl.BlockSpec(memory_space=pltpu.VMEM)
+    hbmspec = pl.BlockSpec(memory_space=pltpu.HBM)
     anyspec = pl.BlockSpec(memory_space=pl.ANY)
     products, gram = pl.pallas_call(
         functools.partial(kernel, n, split, rows, per, total),
-        out_shape=(jax.ShapeDtypeStruct((vecs * BINS, samples), F32),
-                   jax.ShapeDtypeStruct((n, per, LANES), F32)),
-        in_specs=[anyspec] + [vspec] * 5,
-        out_specs=(anyspec, vspec),
+        out_shape=(vm((vecs * BINS, samples), F32), vm((n, per, LANES), F32)),
+        in_specs=[hbmspec] * 6,
+        out_specs=(vspec, vspec),
         scratch_shapes=[
+            vm(probe_signs.shape, jnp.int32),
+            vm((1, samples), F32),
+            vm((1, markers), F32),
+            vm((1, markers), F32),
+            vm((1, markers), jnp.int32),
             vm((groups, samples, GROUP), jnp.int32),
             vm((samples, markers), BF),
             vm((probes + 16, samples), BF),
@@ -326,22 +363,29 @@
             vm((chips, rows, LANES), F32),
             vm((n, rows, LANES), F32),
             vm((2 * vecs * BINS, GROUP), BF),
-            vm((vecs * BINS, samples), F32),
             vm((vecs * BINS, LANES), F32),
             vm((n, per, LANES), F32),
             vm((n, per, LANES), F32),
             vm((n, per, LANES), F32),
-            dma((groups,)), dma((samples // GROUP,)),
+            dma((5,)), dma((groups,)),
             dma((chips,)), dma((chips,)), dma((chips,)), dma((chips,)),
             dma((chips,)), dma((n,)), dma((chips,)),
             dma((n,)), dma((n,)), dma((n,)), dma((n,)),
         ],
         compiler_params=pltpu.CompilerParams(
-            collective_id=0, has_side_effects=True, vmem_limit_bytes=60 * 1024 * 1024),
-    )(genotypes, probe_signs, phenotype[None, :], marker_mean[None, :],
-      marker_scale[None, :], marker_bin[None, :])
-    gram = gram.reshape(n * per, LANES)[:BINS * width].reshape(BINS, width * LANES)
-    gram = gram[:, :vecs * BINS].reshape(BINS, vecs, BINS).transpose(0, 2, 1)
+            collective_id=0, has_side_effects=True, vmem_limit_bytes=32 * 1024 * 1024),
+    )(*[pltpu.with_memory_space_constraint(x, pltpu.HBM) for x in (
+        genotypes, probe_signs, phenotype[None, :], marker_mean[None, :],
+        marker_scale[None, :], marker_bin[None, :])])
+    products, gram = pl.pallas_call(
+        functools.partial(finisher, n, per, width, vecs),
+        out_shape=(jax.ShapeDtypeStruct((vecs * BINS, samples), F32),
+                   jax.ShapeDtypeStruct((BINS, BINS, vecs), F32)),
+        in_specs=[vspec, vspec],
+        out_specs=(anyspec, vspec),
+        scratch_shapes=[dma((3,))],
+        compiler_params=pltpu.CompilerParams(vmem_limit_bytes=16 * 1024 * 1024),
+    )(products, gram)
     return products.reshape(vecs, BINS, samples).transpose(1, 0, 2), gram
 
 

time: 42 us -> 38.6 us (0.919)
  local copies, waits for them, and re-layouts: 5.01 us -> 0 us
  Pallas kernels: 36.1 us -> 37.8 us
    unnamed x3 -> x0, local copies, waits for them, and re-layouts: 4.89 us -> none
    pallas_call x0 -> x1, Pallas kernels: none -> 2.03 us  [shards(): pl.pallas_call(functools.partial(finisher, n, per, width, vecs), out_shap...]
where the time goes in v3:
time: 38.6 us; the launch traced here: 38.4 us
  Pallas kernels  37.8 us (98%)
  between operations  0.64 us (2%)
    pallas_call x1, Pallas kernels, shards(): pl.pallas_call(functools.partial(kernel, n, split, rows, per, total), out...  35.7 us
    pallas_call x1, Pallas kernels, shards(): pl.pallas_call(functools.partial(finisher, n, per, width, vecs), out_shap...  2.03 us

profile of v3, /device:TPU:0, one launch (start us, length us, event | category | flops | bytes accessed | tf_op | source)
XLA Modules:
  0.0 38.4 jit_solution(11684759116158624937)
XLA Ops:
  0.6 35.7 %shard_map.77 = (f32[528,1024]{1,0:T(8,128)S(1)}, f32[16,5,128]{2,1,0:T(8,128)S(1)}) custom-call(s32[1024,2048]{1,0:T(8,128)} %g_hbm.1, s32[32,1024]{1,0:T(8,128)} %probe_hbm.1, f32[1,1024]{1,0:T(1,128)} %bitcast.10, f32[1,2048]{1,0:T(1,128)} %bitcast.7, f32[1,2048]{1,0:T(1,128)} %bitcast.8, s32[1,2048]{1,0:T(1,128)} %bitcast.9), custom_call_target="tpu_custom_call" | custom-call | tf_op jit(solution)/shard_map/pallas_call | solution.py:346
  36.4 2.0 %shard_map.78 = (f32[528,1024]{1,0:T(8,128)}, f32[16,16,33]{2,1,0:T(8,128)}) custom-call(f32[528,1024]{1,0:T(8,128)S(1)} %get-tuple-element.6.prods, f32[16,5,128]{2,1,0:T(8,128)S(1)} %get-tuple-element.7.gsum), custom_call_target="tpu_custom_call" | custom-call | tf_op jit(solution)/shard_map/pallas_call | solution.py:380

commit v4 on v3

--- a/solution.py
+++ b/solution.py
@@ -54,8 +54,14 @@
     def _(s):
         pl.semaphore_signal(barrier, inc=1, device_id={"samp": lax.rem(me + s, n)}, device_id_type=MESH)
 
+    def near(s):
+        if groups & (groups - 1):
+            return lax.rem(home + s, groups)
+        return sum(2 ** b * ((home // 2 ** b + s // 2 ** b) % 2)
+                   for b in range(groups.bit_length() - 1))
+
     def cg_of(q):
-        return lax.rem(home + 1 + q, groups)
+        return near(groups - 1 - q)
 
     def cols(q):
         return pl.ds(pl.multiple_of(cg_of(q) * GROUP, GROUP), GROUP)
@@ -169,7 +175,12 @@
             ag.at[d], ag.at[d], fwd_s.at[chip], ag_r.at[d],
             device_id={"samp": sib}, device_id_type=MESH)
 
-    others(lambda m: ag_chip(m).start())
+    if split == 1:
+        @pl.loop(1, groups)
+        def _(s):
+            ag_chip(near(s)).start()
+    else:
+        others(lambda m: ag_chip(m).start())
     ag_fwd(chip).start()
 
     factor = 1.0 / (math.sqrt(total) * math.sqrt(M_BIN))
@@ -179,7 +190,7 @@
 
     def receive(s):
         for i in range(split):
-            m = lax.rem(home + s, groups) * split + i
+            m = near(s) * split + i
 
             @pl.when(m != chip)
             def _():
@@ -187,7 +198,7 @@
                 ag_fwd(m).start()
 
     def multiply(s):
-        cg = lax.rem(home + s, groups)
+        cg = near(s)
         for i in range(split):
             ag_got(2 * (cg * split + i) + 1 - core).wait_recv()
         at = pl.ds(pl.multiple_of(cg * GROUP, GROUP), GROUP)

time: 38.6 us -> 36.8 us (0.953)
  Pallas kernels: 37.8 us -> 36 us
    pallas_call x1, Pallas kernels: 35.7 us -> 34 us  [shards(): pl.pallas_call(functools.partial(kernel, n, split, rows, per, total), out...]
where the time goes in v4:
time: 36.8 us; the launch traced here: 36.7 us
  Pallas kernels  36 us (98%)
  between operations  0.64 us (2%)
    pallas_call x1, Pallas kernels, shards(): pl.pallas_call(functools.partial(kernel, n, split, rows, per, total), out...  34 us
    pallas_call x1, Pallas kernels, shards(): pl.pallas_call(functools.partial(finisher, n, per, width, vecs), out_shap...  2.03 us

profile of v4, /device:TPU:0, one launch (start us, length us, event | category | flops | bytes accessed | tf_op | source)
XLA Modules:
  0.0 36.7 jit_solution(17195171940940827920)
XLA Ops:
  0.6 34.0 %shard_map.77 = (f32[528,1024]{1,0:T(8,128)S(1)}, f32[16,5,128]{2,1,0:T(8,128)S(1)}) custom-call(s32[1024,2048]{1,0:T(8,128)} %g_hbm.1, s32[32,1024]{1,0:T(8,128)} %probe_hbm.1, f32[1,1024]{1,0:T(1,128)} %bitcast.10, f32[1,2048]{1,0:T(1,128)} %bitcast.7, f32[1,2048]{1,0:T(1,128)} %bitcast.8, s32[1,2048]{1,0:T(1,128)} %bitcast.9), custom_call_target="tpu_custom_call" | custom-call | tf_op jit(solution)/shard_map/pallas_call | solution.py:357
  34.6 2.0 %shard_map.78 = (f32[528,1024]{1,0:T(8,128)}, f32[16,16,33]{2,1,0:T(8,128)}) custom-call(f32[528,1024]{1,0:T(8,128)S(1)} %get-tuple-element.6.prods, f32[16,5,128]{2,1,0:T(8,128)S(1)} %get-tuple-element.7.gsum), custom_call_target="tpu_custom_call" | custom-call | tf_op jit(solution)/shard_map/pallas_call | solution.py:391
